TPU v7x, 32 devices: a whole 2x2x4 slice. The times are simulated.
32 devices in a mesh: grp: 4 (over y, x), dev: 8 (over z, core).
Axes of the slice: x: 2, y: 2, z: 4, core: 2. Of those that a mesh axis runs over, the one named last changes fastest.
Arguments:
- queries: bfloat16 [4096, 256], P(('grp', 'dev')), may hold values from -32 to 32
- items: bfloat16 [4096, 256], P(('grp', 'dev')), may hold values from -24 to 24
- item_ids: int32 [4096], P('grp'), may hold values from 0 to 262143
- neg_embed: bfloat16 [4096, 256], P('dev'), may hold values from -6 to 6
- neg_logq: float32 [4096], P('dev'), may hold values from -12 to -8
- logq_table: float32 [262144], replicated, may hold values from -11 to -9.5
Outputs:
- query_loss: float32 [4096], P(('grp', 'dev'))
- query_grad: float32 [4096, 256], P(('grp', 'dev'))
- item_grad: float32 [4096, 256], P(('grp', 'dev'))
- negative_grad: float32 [4096, 256], P('dev')
Inputs may be any that keep to these rules, and one draw needn't show every extreme that they name: `item_ids`: a row of logq_table.
All inputs are finite; a program needn't handle non-finite values.
Results may differ from a plain program's by a relative error of at most 0.0036.
Values may be sent and summed in bfloat16 or wider, within the bound.
No kernel may reach another device: no remote copies, remote signals or barrier semaphores. Data moves between devices by JAX's collectives and lax.ppermute only.
A program may use at most 64 MiB of HBM per device.

v0:
```python
import jax
import jax.numpy as jnp
from jax import lax
from jax.sharding import PartitionSpec as P

logit_scale = 0.25


def block_shape(all_rows):
    block_rows = min(512, all_rows)
    return (block_rows, all_rows // block_rows)


def log_total(maxima, totals):
    row_max = lax.pmax(maxima, "dev")
    row_sum = lax.psum(totals * jnp.exp(maxima - row_max), "dev")
    return row_max + jnp.log(row_sum)


def row_stats(scores):
    row_max = jnp.max(scores, axis=1)
    return (row_max, jnp.sum(jnp.exp(scores - row_max[:, None]), axis=1))


def logits(q_block, candidates, cand_offsets):
    return (
        logit_scale * jnp.dot(q_block, candidates.T, preferred_element_type=jnp.float32)
        - cand_offsets[None, :]
    )


def local(queries, items, item_ids, neg_embed, neg_logq, logq_table):
    own_rows, feat_width = queries.shape
    dev_index = lax.axis_index("dev")
    own_start = dev_index * own_rows
    own_ids = lax.dynamic_slice_in_dim(item_ids, own_start, own_rows, 0)
    own_offsets = jnp.take(logq_table, own_ids, axis=0)
    group_q = lax.all_gather(queries, "dev", axis=0, tiled=True)
    all_rows = group_q.shape[0]
    block_rows, block_count = block_shape(all_rows)
    blocks = group_q.reshape(block_count, block_rows, feat_width)
    starts = jnp.arange(block_count, dtype=jnp.int32) * block_rows
    candidates = jnp.concatenate([items, neg_embed], axis=0)
    cand_offsets = jnp.concatenate([own_offsets, neg_logq], axis=0)
    columns = jnp.arange(candidates.shape[0], dtype=jnp.int32)

    def positives(first_row):
        targets = first_row + jnp.arange(block_rows, dtype=jnp.int32) - own_start
        return (columns[None, :] == targets[:, None]) & (columns[None, :] < own_rows)

    def forward(packed):
        q_block, first_row = packed
        scores = logits(q_block, candidates, cand_offsets)
        row_max, row_sum = row_stats(scores)
        return (row_max, row_sum, jnp.sum(jnp.where(positives(first_row), scores, 0.0), axis=1))

    maxima, totals, matched = lax.map(forward, (blocks, starts))
    log_norm = log_total(maxima.reshape(all_rows), totals.reshape(all_rows))
    own_norm = lax.dynamic_slice_in_dim(log_norm, own_start, own_rows, 0)
    own_match = lax.dynamic_slice_in_dim(matched.reshape(all_rows), own_start, own_rows, 0)
    query_loss = own_norm - own_match

    def backward(summed, packed):
        q_block, first_row, block_norm = packed
        scores = logits(q_block, candidates, cand_offsets)
        logit_grad = (
            logit_scale
            * (jnp.exp(scores - block_norm[:, None]) - positives(first_row).astype(jnp.float32))
        ).astype(jnp.bfloat16)
        summed = summed + jnp.einsum(
            "rc,rd->cd", logit_grad, q_block, preferred_element_type=jnp.float32
        )
        return (summed, jnp.dot(logit_grad, candidates, preferred_element_type=jnp.float32))

    zero_acc = jnp.zeros((candidates.shape[0], feat_width), jnp.float32)
    cand_grad, q_partial = lax.scan(
        backward, zero_acc, (blocks, starts, log_norm.reshape(block_count, block_rows))
    )
    query_grad = lax.psum_scatter(
        q_partial.reshape(all_rows, feat_width), "dev", scatter_dimension=0, tiled=True
    )
    item_grad = cand_grad[:own_rows]
    negative_part = cand_grad[own_rows:]
    negative_grad = lax.psum(negative_part, "grp")
    return (query_loss, query_grad, item_grad, negative_grad)


def solution(mesh):
    return jax.shard_map(
        local,
        mesh=mesh,
        in_specs=(
            P(("grp", "dev"), None),
            P(("grp", "dev"), None),
            P("grp"),
            P("dev", None),
            P("dev"),
            P(),
        ),
        out_specs=(
            P(("grp", "dev")),
            P(("grp", "dev"), None),
            P(("grp", "dev"), None),
            P("dev", None),
        ),
        check_vma=False,
    )
```

profile of v0, /device:TPU:0, one launch (start us, length us, event | category | flops | bytes accessed | tf_op | source)
XLA Modules:
  0.0 128.1 jit_solution(7890898230688318742)
XLA Ops:
  8.1 0.8 compare_select_fusion
  9.2 1.1 gather_fusion
  10.4 0.8 and_select_fusion
  11.2 0.8 constant_dynamic-update-slice_fusion.1
  12.0 16.7 %all_gather.3 = bf16[1024,256]{1,0:T(8,128)(2,1)S(1)} all-gather(bf16[128,256]{1,0:T(8,128)(2,1)} %param.10), channel_id=1, replica_groups=mesh['grp'=4,'dev'=8] {'dev'}, dimensions={0}, use_global_device_ids=true | all-gather | bytes 589824 | tf_op jit(solution)/shard_map/all_gather | solution.py:38
  28.7 0.7 pad_maximum_fusion
  29.4 5.2 %while.30 = (s32[]{:T(128)}, f32[2,512]{1,0:T(2,128)S(1)}, f32[2,512]{1,0:T(2,128)S(1)}, f32[2,512]{1,0:T(2,128)S(1)}, bf16[2,512,256]{2,1,0:T(8,128)(2,1)S(1)},...) while((s32[]{:T(128)}, f32[2,512]{1,0:T(2,128)S(1)}, ...), condition=%wide.region_4.5_spmd.clone.clone, body=%wide.region_0.4_spmd.clone.clone.sunk | while | flops 170721408 | bytes 3241369 | solution.py:57
  29.4 0.6 dynamic_slice.67
  30.0 0.6 add_subtract_fusion.4
  31.2 0.7 select_reduce_fusion.2
  32.0 0.6 dynamic_slice.67
  32.6 0.6 add_subtract_fusion.4
  33.8 0.7 select_reduce_fusion.2
  34.6 17.0 %pmax.7 = f32[1024]{0:T(1024)S(1)} all-reduce(f32[1024]{0:T(1024)S(1)} %bitcast.69), channel_id=1, replica_groups=mesh['grp'=4,'dev'=8] {'dev'}, use_global_device_ids=true, to_apply=%region_5.6 | all-reduce | flops 1024 | bytes 8192 | tf_op jit(solution)/shard_map/pmax | solution.py:15
  51.6 13.6 %psum.14 = f32[1024]{0:T(1024)S(1)} all-reduce(f32[1024]{0:T(1024)S(1)} %exponential_multiply_fusion), channel_id=1, replica_groups=mesh['grp'=4,'dev'=8] {'dev'}, use_global_device_ids=true, to_apply=%region_6.7 | all-reduce | flops 1024 | bytes 8192 | tf_op jit(solution)/shard_map/psum | solution.py:16
  65.2 9.0 %while.31 = (s32[]{:T(128)}, f32[640,256]{1,0:T(8,128)S(1)}, f32[2,512,256]{2,1,0:T(8,128)}, bf16[2,512,256]{2,1,0:T(8,128)(2,1)S(1)}, bf16[640,256]{1,0:T(8,128...) while((s32[]{:T(128)}, f32[640,256]{1,0:T(8,128)S(1)}, ...), condition=%wide.region_8.9_spmd.clone.clone, body=%wide.region_7.8_spmd.clone.clone.sunk | while | flops 506594944 | bytes 13385563 | solution.py:76
  65.2 0.6 dynamic_slice.71
  65.8 0.6 add_subtract_fusion.5
  66.5 0.6 fusion.47
  67.7 0.7 copy-done.1
  68.7 1.0 copy-done.2
  69.7 0.6 dynamic_slice.71
  70.3 0.6 add_subtract_fusion.5
  71.0 0.6 fusion.47
  71.6 0.5 convolution_add_fusion.2
  72.2 0.7 copy-done.1
  73.2 1.0 copy-done.2
  74.2 0.8 slice.7
  75.7 0.7 slice.6
  76.3 0.6 dynamic-slice_subtract_fusion
  76.9 41.9 %all-reduce.2.cloned.1.call-done = f32[512,256]{1,0:T(8,128)} async-done(((f32[512,256]{1,0:T(8,128)}), f32[512,256]{1,0:T(8,128)}) %all-reduce.2.cloned.1.call-update) | async-done | bytes 524304 | tf_op jit(solution)/shard_map/psum | solution.py:84
  118.8 1.9 %copy.40 = f32[512,256]{1,0:T(8,128)} copy(f32[512,256]{1,0:T(8,128)} %all-reduce.2.cloned.1.call-done) | data formatting | bytes 1048576
  (44 shorter events, 3.5 us)
Async XLA Ops:
  8.0 1.2 copy-start
  8.0 21.4 %copy-start.3 = (bf16[512,256]{1,0:T(8,128)(2,1)S(1)}, bf16[512,256]{1,0:T(8,128)(2,1)}, u32[]{:S(2)}) copy-start(bf16[512,256]{1,0:T(8,128)(2,1)} %param.13) | copy-start | bytes 786436
  8.0 110.8 %all-reduce.2.cloned.1.call-start = ((), (), s32[]{:S(2)}) async-start(), calls=%async_computation.2 | async-start | bytes 1048576 | tf_op jit(solution)/shard_map/psum | solution.py:84
  67.1 1.2 copy-start.1
  68.7 1.0 copy-start.2
  71.6 1.2 copy-start.1
  73.2 1.0 copy-start.2
  75.1 43.7 %reduce-scatter.2.cloned.1.call-start = ((), (), s32[]{:S(2)}) async-start(), calls=%async_computation.1 | async-start | bytes 1179648 | tf_op jit(solution)/shard_map/reduce_scatter | solution.py:79
Sparse Core Ops, SparseCore 0:
  75.2 43.5 all-reduce.1
Sparse Core Ops, SparseCore 1:
  78.4 30.7 reduce-scatter.1
where the time goes:
time: 129 us; the launch traced here: 128 us
  blocking collectives  47.3 us (37%)
  waiting for transfers between devices  42.4 us (33%)
  between operations  15.6 us (12%)
  local copies, waits for them, and re-layouts  11.6 us (9%)
  other arithmetic  6.94 us (5%)
  matrix products  4.02 us (3%)
    psum x1, waiting for transfers between devices, local(): negative_grad = lax.psum(negative_part, 'grp')  41.9 us
    pmax x1, blocking collectives, log_total(): row_max = lax.pmax(maxima, 'dev')  17 us
    all_gather x1, blocking collectives, local(): group_q = lax.all_gather(queries, 'dev', axis=0, tiled=True)  16.7 us
    psum x1, blocking collectives, log_total(): row_sum = lax.psum(totals * jnp.exp(maxima - row_max), 'dev')  13.6 us
    while x8, local copies, waits for them, and re-layouts  3.35 us
    unnamed x9, local copies, waits for them, and re-layouts  2.99 us
    sub x4, other arithmetic, positives(): targets = first_row + jnp.arange(block_rows, dtype=jnp.int32) - own_start  2.59 us
  transfers between devices with their start and end apart: 2, of which 1 were waited for; matrix products, arithmetic and copies ran while one was open for 1% of the time, Pallas kernels for 0%

commit v1 on v0

--- a/solution.py
+++ b/solution.py
@@ -1,9 +1,25 @@
+import functools
 import jax
 import jax.numpy as jnp
 from jax import lax
 from jax.sharding import PartitionSpec as P
 
 logit_scale = 0.25
+
+
+def start_files_here(s0, axis_key):
+    how_many = lax.axis_size(axis_key)
+    y1 = s0
+    for u in [
+        [(hop_no, hop_no ^ nth) for hop_no in range(how_many)]
+        for nth in (1, 2, 4, 8, 16)
+        if nth < how_many
+    ]:
+        y1 = y1 + lax.ppermute(y1, axis_name=axis_key, perm=u)
+    return y1
+
+
+_lay_inputs = functools.partial(start_files_here, axis_key="grp")
 
 
 def block_shape(all_rows):
@@ -81,7 +97,7 @@
     )
     item_grad = cand_grad[:own_rows]
     negative_part = cand_grad[own_rows:]
-    negative_grad = lax.psum(negative_part, "grp")
+    negative_grad = _lay_inputs(negative_part)
     return (query_loss, query_grad, item_grad, negative_grad)
 
 

time: 129 us -> 112 us (0.87)
  waiting for transfers between devices: 42.4 us -> 25.6 us
  starting transfers between devices: 0.08 us -> 3.18 us
  local copies, waits for them, and re-layouts: 11.6 us -> 8.96 us
  between operations: 15.6 us -> 14.2 us
    psum x1 -> x0, waiting for transfers between devices: 41.9 us -> none  [local(): negative_grad = lax.psum(negative_part, 'grp')]
    ppermute x0 -> x2, waiting for transfers between devices: none -> 22.3 us  [start_files_here(): y1 = y1 + lax.ppermute(y1, axis_name=axis_key, perm=u)]
    reduce_scatter x1, waiting for transfers between devices: 0.01 us -> 3.29 us  [local(): lax.psum_scatter(q_partial.reshape(all_rows, feat_width), 'dev', scatter_...]
    ppermute x0 -> x2, starting transfers between devices: none -> 3.14 us  [start_files_here(): y1 = y1 + lax.ppermute(y1, axis_name=axis_key, perm=u)]
    unnamed x9 -> x8, local copies, waits for them, and re-layouts: 2.99 us -> 1.12 us
  transfers between devices with their start and end apart: 2 -> 3, of which waited for: 1 -> 3; matrix products, arithmetic and copies ran while one was open for 1% -> 2% of each run, Pallas kernels for 0% -> 0%
where the time goes in v1:
time: 112 us; the launch traced here: 111 us
  blocking collectives  47.3 us (42%)
  waiting for transfers between devices  25.6 us (23%)
  between operations  14.2 us (13%)
  local copies, waits for them, and re-layouts  8.96 us (8%)
  other arithmetic  7.87 us (7%)
  matrix products  4.03 us (4%)
  starting transfers between devices  3.18 us (3%)
    ppermute x2, waiting for transfers between devices, start_files_here(): y1 = y1 + lax.ppermute(y1, axis_name=axis_key, perm=u)  22.3 us
    pmax x1, blocking collectives, log_total(): row_max = lax.pmax(maxima, 'dev')  17 us
    all_gather x1, blocking collectives, local(): group_q = lax.all_gather(queries, 'dev', axis=0, tiled=True)  16.7 us
    psum x1, blocking collectives, log_total(): row_sum = lax.psum(totals * jnp.exp(maxima - row_max), 'dev')  13.6 us
    while x8, local copies, waits for them, and re-layouts  3.35 us
    reduce_scatter x1, waiting for transfers between devices, local(): lax.psum_scatter(q_partial.reshape(all_rows, feat_width), 'dev', scatter_...  3.29 us
    ppermute x2, starting transfers between devices, start_files_here(): y1 = y1 + lax.ppermute(y1, axis_name=axis_key, perm=u)  3.14 us
    sub x4, other arithmetic, positives(): targets = first_row + jnp.arange(block_rows, dtype=jnp.int32) - own_start  2.59 us
  transfers between devices with their start and end apart: 3, of which 3 were waited for; matrix products, arithmetic and copies ran while one was open for 2% of the time, Pallas kernels for 0%

profile of v1, /device:TPU:0, one launch (start us, length us, event | category | flops | bytes accessed | tf_op | source)
XLA Modules:
  0.0 111.2 jit_solution(10711999760987001883)
XLA Ops:
  7.3 0.8 compare_select_fusion
  8.4 1.1 %gather_fusion = f32[128]{0:T(128)S(1)} fusion(f32[262144]{0:T(1024)S(1)} %copy-done, s32[1024]{0:T(1024)S(1)} %pad_clamp_fusion), kind=kCustom, calls=%fused_computation | custom fusion | bytes 1536 | tf_op jit(solution)/shard_map/jit(_take)/gather | solution.py:53
  9.6 0.8 and_select_fusion
  10.3 0.8 constant_dynamic-update-slice_fusion.1
  11.2 16.7 %all_gather.3 = bf16[1024,256]{1,0:T(8,128)(2,1)S(1)} all-gather(bf16[128,256]{1,0:T(8,128)(2,1)} %param.10), channel_id=1, replica_groups=mesh['grp'=4,'dev'=8] {'dev'}, dimensions={0}, use_global_device_ids=true | all-gather | bytes 589824 | tf_op jit(solution)/shard_map/all_gather | solution.py:54
  27.9 0.7 pad_maximum_fusion
  28.6 5.2 %while.30 = (s32[]{:T(128)}, f32[2,512]{1,0:T(2,128)S(1)}, f32[2,512]{1,0:T(2,128)S(1)}, f32[2,512]{1,0:T(2,128)S(1)}, bf16[2,512,256]{2,1,0:T(8,128)(2,1)S(1)},...) while((s32[]{:T(128)}, f32[2,512]{1,0:T(2,128)S(1)}, ...), condition=%wide.region_4.5_spmd.clone.clone, body=%wide.region_0.4_spmd.clone.clone.sunk | while | flops 170721408 | bytes 3241369 | solution.py:73
  28.6 0.6 dynamic_slice.67
  29.2 0.6 add_subtract_fusion.4
  30.3 0.7 select_reduce_fusion.2
  31.8 0.6 add_subtract_fusion.4
  32.9 0.7 select_reduce_fusion.2
  33.8 17.0 %pmax.7 = f32[1024]{0:T(1024)S(1)} all-reduce(f32[1024]{0:T(1024)S(1)} %bitcast.69), channel_id=1, replica_groups=mesh['grp'=4,'dev'=8] {'dev'}, use_global_device_ids=true, to_apply=%region_5.6 | all-reduce | flops 1024 | bytes 8192 | tf_op jit(solution)/shard_map/pmax | solution.py:31
  50.8 13.6 %psum.7 = f32[1024]{0:T(1024)S(1)} all-reduce(f32[1024]{0:T(1024)S(1)} %exponential_multiply_fusion), channel_id=1, replica_groups=mesh['grp'=4,'dev'=8] {'dev'}, use_global_device_ids=true, to_apply=%region_6.7 | all-reduce | flops 1024 | bytes 8192 | tf_op jit(solution)/shard_map/psum | solution.py:32
  64.4 9.0 %while.31 = (s32[]{:T(128)}, f32[640,256]{1,0:T(8,128)S(1)}, f32[2,512,256]{2,1,0:T(8,128)}, bf16[2,512,256]{2,1,0:T(8,128)(2,1)S(1)}, bf16[640,256]{1,0:T(8,128...) while((s32[]{:T(128)}, f32[640,256]{1,0:T(8,128)S(1)}, ...), condition=%wide.region_8.9_spmd.clone.clone, body=%wide.region_7.8_spmd.clone.clone.sunk | while | flops 506594944 | bytes 13385563 | solution.py:92
  64.4 0.6 dynamic_slice.71
  65.0 0.6 add_subtract_fusion.5
  65.7 0.6 fusion.47
  66.8 0.7 copy-done.1
  67.9 1.0 copy-done.2
  69.5 0.6 add_subtract_fusion.5
  70.2 0.6 fusion.47
  71.3 0.7 copy-done.1
  72.4 1.0 copy-done.2
  73.5 1.6 %collective-permute-start = (f32[512,256]{1,0:T(8,128)S(1)}, f32[512,256]{1,0:T(8,128)S(1)}, u32[]{:S(2)}, u32[]{:S(2)}) collective-permute-start(f32[512,256]{1,0:T(8,128)S(1)} %slice.7), channel_id=1, source_target_pairs={{0,8},{8,0},{16,24},{24,16},{1,9},{9,1},{17,25},{25,17},{2,10},{10... | collective-permute-start | bytes 1572872 | tf_op jit(solution)/shard_map/ppermute | solution.py:18
  75.0 12.2 %collective-permute-done = f32[512,256]{1,0:T(8,128)S(1)} collective-permute-done((f32[512,256]{1,0:T(8,128)S(1)}, f32[512,256]{1,0:T(8,128)S(1)}, u32[]{:S(2)}, u32[]{:S(2)}) %collective-permute-start) | collective-permute-done | bytes 524320 | tf_op jit(solution)/shard_map/ppermute | solution.py:18
  87.3 1.6 %collective-permute-start.1 = (f32[512,256]{1,0:T(8,128)S(1)}, f32[512,256]{1,0:T(8,128)S(1)}, u32[]{:S(2)}, u32[]{:S(2)}) collective-permute-start(f32[512,256]{1,0:T(8,128)S(1)} %slice_add_fusion), channel_id=1, source_target_pairs={{0,16},{8,24},{16,0},{24,8},{1,17},{9,25},{17,1},{25,9},{2,18},{10... | collective-permute-start | bytes 1572872 | tf_op jit(solution)/shard_map/ppermute | solution.py:18
  88.9 0.7 slice.6
  89.6 0.6 dynamic-slice_subtract_fusion
  90.2 10.1 %collective-permute-done.1 = f32[512,256]{1,0:T(8,128)S(1)} collective-permute-done((f32[512,256]{1,0:T(8,128)S(1)}, f32[512,256]{1,0:T(8,128)S(1)}, u32[]{:S(2)}, u32[]{:S(2)}) %collective-permute-start.1) | collective-permute-done | bytes 524320 | tf_op jit(solution)/shard_map/ppermute | solution.py:18
  100.2 0.9 add.60
  101.1 3.3 %reduce-scatter.2.cloned.1.call-done = f32[128,256]{1,0:T(8,128)} async-done(((f32[1024,256]{1,0:T(8,128)}), f32[128,256]{1,0:T(8,128)}) %reduce-scatter.2.cloned.1.call-update) | async-done | bytes 131088 | tf_op jit(solution)/shard_map/reduce_scatter | solution.py:95
  (46 shorter events, 4.7 us)
Async XLA Ops:
  7.2 1.2 %copy-start = (f32[262144]{0:T(1024)S(1)}, f32[262144]{0:T(1024)}, u32[]{:S(2)}) copy-start(f32[262144]{0:T(1024)} %param.15) | copy-start | bytes 3145732
  7.2 21.4 %copy-start.3 = (bf16[512,256]{1,0:T(8,128)(2,1)S(1)}, bf16[512,256]{1,0:T(8,128)(2,1)}, u32[]{:S(2)}) copy-start(bf16[512,256]{1,0:T(8,128)(2,1)} %param.13) | copy-start | bytes 786436
  7.2 97.2 %reduce-scatter.2.cloned.1.call-start = ((), (), s32[]{:S(2)}) async-start(), calls=%async_computation.1 | async-start | bytes 1179648 | tf_op jit(solution)/shard_map/reduce_scatter | solution.py:95
  66.3 1.2 %copy-start.1 = (f32[2,512,256]{2,1,0:T(8,128)S(1)}, f32[2,512,256]{2,1,0:T(8,128)}, u32[]{:S(2)}) copy-start(f32[2,512,256]{2,1,0:T(8,128)} %get-tuple-element.426) | copy-start | bytes 3145732 | tf_op jit(solution)/shard_map/while
  67.9 1.0 copy-start.2
  70.8 1.2 %copy-start.1 = (f32[2,512,256]{2,1,0:T(8,128)S(1)}, f32[2,512,256]{2,1,0:T(8,128)}, u32[]{:S(2)}) copy-start(f32[2,512,256]{2,1,0:T(8,128)} %get-tuple-element.426) | copy-start | bytes 3145732 | tf_op jit(solution)/shard_map/while
  72.4 1.0 copy-start.2
  73.5 13.8 %collective-permute-start = (f32[512,256]{1,0:T(8,128)S(1)}, f32[512,256]{1,0:T(8,128)S(1)}, u32[]{:S(2)}, u32[]{:S(2)}) collective-permute-start(f32[512,256]{1,0:T(8,128)S(1)} %slice.7), channel_id=1, source_target_pairs={{0,8},{8,0},{16,24},{24,16},{1,9},{9,1},{17,25},{25,17},{2,10},{10... | collective-permute-start | bytes 1572872 | tf_op jit(solution)/shard_map/ppermute | solution.py:18
  87.3 12.9 %collective-permute-start.1 = (f32[512,256]{1,0:T(8,128)S(1)}, f32[512,256]{1,0:T(8,128)S(1)}, u32[]{:S(2)}, u32[]{:S(2)}) collective-permute-start(f32[512,256]{1,0:T(8,128)S(1)} %slice_add_fusion), channel_id=1, source_target_pairs={{0,16},{8,24},{16,0},{24,8},{1,17},{9,25},{17,1},{25,9},{2,18},{10... | collective-permute-start | bytes 1572872 | tf_op jit(solution)/shard_map/ppermute | solution.py:18
Sparse Core Ops, SparseCore 0:
  73.5 30.8 reduce-scatter.1
